TPU v7x, 256 devices: a whole 4x4x8 slice. The times are simulated.
256 devices in a mesh: orb: 16 (over y, x), aux: 16 (over z, core).
Axes of the slice: x: 4, y: 4, z: 8, core: 2. Of those that a mesh axis runs over, the one named last changes fastest.
Arguments:
- b_rows: bfloat16 [4096, 128, 8, 128], P('aux', 'orb'), may hold values from -6 to 6
- col_blocks: int32 [16, 8], P('orb'), may hold values from 0 to 15, all different within a row
- g_occ: bfloat16 [2, 128, 128], P(None, 'orb'), may hold values from -0.5 to 0.5
- occ_live: int32 [2, 16, 16], replicated, may hold values 0 or 1
- g_virt: bfloat16 [2, 16, 128, 128], P(None, 'orb', 'aux'), may hold values from -0.5 to 0.5
- tau_weight: float32 [2], replicated, may hold values from 0.5 to 2
Outputs:
- chi: float32 [256, 4096], P('orb', 'aux')
Inputs may be any that keep to these rules, and one draw needn't show every extreme that they name: `col_blocks`: each row group lists 8 different column blocks, and every column block is listed by some row group.
All inputs are finite; a program needn't handle non-finite values.
Results may differ from a plain program's by a relative error of at most 0.0041.
Values may be sent and summed in bfloat16 or wider, within the bound.
A program may use at most 128 MiB of HBM per device.

v0:
```python
import math

import jax
import jax.numpy as jnp
from jax import lax
from jax.sharding import PartitionSpec as P


def on_device(b_rows, col_blocks, g_occ, occ_live, g_virt, tau_weight):
    orb_count = lax.axis_size("orb")
    aux_dev, rows_dev, slot_count, tile_width = b_rows.shape
    tau_count = g_occ.shape[0]
    picked = (col_blocks[0][:, None] == jnp.arange(orb_count, dtype=jnp.int32)[None, :]).astype(
        jnp.bfloat16
    )
    outgoing = jnp.einsum("prkc,kd->prdc", b_rows, picked)
    occ_full = lax.all_gather(g_occ, "orb", axis=1, tiled=True)
    total_rows = occ_full.shape[1]
    live_mask = jnp.repeat(jnp.repeat(occ_live, rows_dev, axis=1), rows_dev, axis=2).astype(
        jnp.bfloat16
    )
    occ_masked = occ_full * live_mask
    virt_block = lax.all_gather(g_virt, "aux", axis=2, tiled=True)
    col_dense = lax.all_to_all(outgoing, "orb", split_axis=2, concat_axis=1, tiled=True).reshape(
        aux_dev, total_rows, tile_width
    )
    virt_list = []
    for moment in range(tau_count):
        product = jnp.dot(
            col_dense.reshape(aux_dev * total_rows, tile_width),
            virt_block[moment, 0],
            preferred_element_type=jnp.float32,
        )
        virt_list.append(product.astype(jnp.bfloat16).reshape(aux_dev, total_rows, tile_width))
    partial_value = jnp.zeros((aux_dev, aux_dev), jnp.float32)
    for moment in range(tau_count):
        occ_prod = jnp.einsum(
            "mn,qnc->qmc", occ_masked[moment], col_dense, preferred_element_type=jnp.float32
        ).astype(jnp.bfloat16)
        term = jnp.einsum(
            "pmc,qmc->qp", virt_list[moment], occ_prod, preferred_element_type=jnp.float32
        )
        partial_value = partial_value + tau_weight[moment] * term
    partial_value = partial_value * (1.0 / math.sqrt(total_rows * tile_width * orb_count))
    whole_sum = lax.psum(partial_value, "orb")
    share_rows = aux_dev // orb_count
    share = lax.dynamic_slice_in_dim(whole_sum, lax.axis_index("orb") * share_rows, share_rows, 0)
    return share


def solution(mesh):
    in_specs = (
        P("aux", "orb", None, None),
        P("orb", None),
        P(None, "orb", None),
        P(),
        P(None, "orb", "aux", None),
        P(),
    )
    out_specs = P("orb", "aux")
    return jax.shard_map(
        on_device, mesh=mesh, in_specs=in_specs, out_specs=out_specs, check_vma=False
    )
```

profile of v0, /device:TPU:2, one launch (start us, length us, event | category | flops | bytes accessed | tf_op | source)
XLA Modules:
  0.0 368.9 jit_solution(9843376873879229038)
XLA Ops:
  6.5 6.3 %convolution_bitcast_fusion = bf16[256,8,16,128]{3,2,1,0:T(8,128)(2,1)} fusion(bf16[256,8,8,128]{3,2,1,0:T(8,128)(2,1)} %param.6, s32[8]{0:T(128)} %bitcast.83), kind=kOutput, calls=%fused_computation.8 | convolution fusion | flops 67108992 | bytes 12582944 | tf_op jit(solution)/shard_map/prkc,kd->prdc/dot_general | solution.py:16
  12.8 8.8 %copy.23 = bf16[256,8,16,128]{3,1,0,2:T(8,128)(2,1)} copy(bf16[256,8,16,128]{3,2,1,0:T(8,128)(2,1)} %convolution_bitcast_fusion) | data formatting | bytes 16777216 | tf_op jit(solution)/shard_map/prkc,kd->prdc/transpose | solution.py:16
  21.6 7.6 %all-to-all-start = ((bf16[256,8,16,128]{3,1,0,2:T(8,128)(2,1)}), bf16[256,8,16,128]{3,1,0,2:T(8,128)(2,1)}, u32[]{:S(2)}, u32[]{:S(2)}) async-start(bf16[256,8,16,128]{3,1,0,2:T(8,128)(2,1)} %copy.23), calls=%async_computation | async-start | bytes 16777216 | tf_op jit(solution)/shard_map/all_to_all | solution.py:24
  29.2 0.0 all-reduce.2.cloned.1.call-start
  29.3 0.0 copy-done.1
  29.3 0.1 copy.25
  29.4 0.1 copy.26
  29.5 0.0 copy-done.2
  29.5 137.6 %all_gather.6 = bf16[2,128,128]{2,1,0:T(8,128)(2,1)S(1)} all-gather(bf16[2,8,128]{2,1,0:T(8,128)(2,1)S(1)} %copy-done.2), channel_id=1, replica_groups=mesh['orb'=16,'aux'=16] {'orb'}, dimensions={1}, use_global_device_ids=true | all-gather | bytes 69632 | tf_op jit(solution)/shard_map/all_gather | solution.py:17
  167.1 0.0 copy-done.3
  167.2 20.1 %all_gather.7 = bf16[2,1,128,128]{3,2,1,0:T(8,128)(2,1)S(1)} all-gather(bf16[2,1,8,128]{3,2,1,0:T(8,128)(2,1)S(1)} %copy-done.3), channel_id=1, replica_groups=mesh['orb'=16,'aux'=16] {'aux'}, dimensions={2}, use_global_device_ids=true | all-gather | bytes 69632 | tf_op jit(solution)/shard_map/all_gather | solution.py:23
  187.3 0.6 fusion.31
  187.9 0.0 all-to-all-done
  187.9 9.0 %copy.34 = bf16[256,8,16,128]{3,1,2,0:T(8,128)(2,1)} copy(bf16[256,8,16,128]{3,1,0,2:T(8,128)(2,1)} %all-to-all-done) | data formatting | bytes 16777216 | tf_op jit(solution)/shard_map/all_to_all | solution.py:24
  196.9 9.1 %convolution_convert_fusion = bf16[32768,128]{1,0:T(8,128)(2,1)} fusion(bf16[32768,128]{1,0:T(8,128)(2,1)} %bitcast.78, bf16[2,1,128,128]{3,2,1,0:T(8,128)(2,1)S(1)} %all_gather.7), kind=kOutput, calls=%fused_computation | convolution fusion | flops 1077936128 | bytes 16809984 | tf_op jit(solution)/shard_map/dot_general | solution.py:29
  206.0 4.5 %convolution_convert_fusion.1 = bf16[32768,128]{1,0:T(8,128)(2,1)} fusion(bf16[32768,128]{1,0:T(8,128)(2,1)S(1)} %bitcast.80, bf16[2,1,128,128]{3,2,1,0:T(8,128)(2,1)S(1)} %all_gather.7), kind=kOutput, calls=%fused_computation.1 | convolution fusion | flops 1077936128 | bytes 16809984 | tf_op jit(solution)/shard_map/dot_general | solution.py:29
  210.5 11.8 %copy.30 = bf16[256,128,128]{1,0,2:T(8,128)(2,1)} copy(bf16[256,128,128]{2,1,0:T(8,128)(2,1)} %bitcast.82) | data formatting | bytes 16777216 | tf_op jit(solution)/shard_map/reshape | solution.py:34
  222.3 11.8 %copy.27 = bf16[256,128,128]{1,0,2:T(8,128)(2,1)} copy(bf16[256,128,128]{2,1,0:T(8,128)(2,1)} %bitcast.79) | data formatting | bytes 16777216 | tf_op jit(solution)/shard_map/reshape | solution.py:24
  234.1 12.3 %copy.28 = bf16[256,128,128]{1,0,2:T(8,128)(2,1)} copy(bf16[256,128,128]{2,1,0:T(8,128)(2,1)} %bitcast.81) | data formatting | bytes 16777216 | tf_op jit(solution)/shard_map/reshape | solution.py:34
  246.4 11.0 %fusion.16 = f32[256,256]{1,0:T(8,128)S(1)} fusion(bf16[256,128,128]{1,0,2:T(8,128)(2,1)} %copy.30, bf16[256,128,128]{1,0,2:T(8,128)(2,1)} %copy.27, f32[]{:T(128)} %bitcast.18, bf16[2,128,128]{2,1,0:T(8,128)(2,1)S(1)} %mul.25), kind=kOutput, calls=%fused_computation.13 | convolution fusion | flops 3225485312 | bytes 17072132 | tf_op jit(solution)/shard_map/pmc,qmc->qp/dot_general | solution.py:40
  257.5 11.8 %fusion.25 = f32[256,256]{1,0:T(8,128)} fusion(f32[256,256]{1,0:T(8,128)S(1)} %fusion.16, bf16[256,128,128]{1,0,2:T(8,128)(2,1)} %copy.28, bf16[256,128,128]{1,0,2:T(8,128)(2,1)} %copy.27, f32[]{:T(128)} %bitcast, bf16[2,128,128]{2,1,0:T(8,128)(2,1)S(1)} %mul.25), kind=kOutput, calls=%fused_computation.16 | convolution fusion | flops 3225616384 | bytes 17334276 | tf_op jit(solution)/shard_map/pmc,qmc->qp/dot_general | solution.py:40
  269.3 0.0 all-reduce.2.cloned.1.call-update
  269.3 91.4 %all-reduce.2.cloned.1.call-done = f32[256,256]{1,0:T(8,128)} async-done(((f32[256,256]{1,0:T(8,128)}), f32[256,256]{1,0:T(8,128)}) %all-reduce.2.cloned.1.call-update) | async-done | bytes 262160 | tf_op jit(solution)/shard_map/psum | solution.py:45
  360.7 1.3 constant_dynamic-slice_fusion
  (11 shorter events, 0.1 us)
Async XLA Ops:
  21.6 7.7 %copy-start.1 = (s32[2,16,16]{2,1,0:T(8,128)S(1)}, s32[2,16,16]{2,1,0:T(8,128)}, u32[]{:S(2)}) copy-start(s32[2,16,16]{2,1,0:T(8,128)} %param.9) | copy-start | bytes 6148
  21.6 8.0 %copy-start.2 = (bf16[2,8,128]{2,1,0:T(8,128)(2,1)S(1)}, bf16[2,8,128]{2,1,0:T(8,128)(2,1)}, u32[]{:S(2)}) copy-start(bf16[2,8,128]{2,1,0:T(8,128)(2,1)} %param.8) | copy-start | bytes 12292
  21.6 145.6 %copy-start.3 = (bf16[2,1,8,128]{3,2,1,0:T(8,128)(2,1)S(1)}, bf16[2,1,8,128]{3,2,1,0:T(8,128)(2,1)}, u32[]{:S(2)}) copy-start(bf16[2,1,8,128]{3,2,1,0:T(8,128)(2,1)} %param.10) | copy-start | bytes 12292
  21.6 165.7 %copy-start.4 = (f32[2]{0:T(128)S(1)}, f32[2]{0:T(128)}, u32[]{:S(2)}) copy-start(f32[2]{0:T(128)} %param.11) | copy-start | bytes 28
  21.6 166.3 %all-to-all-start = ((bf16[256,8,16,128]{3,1,0,2:T(8,128)(2,1)}), bf16[256,8,16,128]{3,1,0,2:T(8,128)(2,1)}, u32[]{:S(2)}, u32[]{:S(2)}) async-start(bf16[256,8,16,128]{3,1,0,2:T(8,128)(2,1)} %copy.23), calls=%async_computation | async-start | bytes 16777216 | tf_op jit(solution)/shard_map/all_to_all | solution.py:24
  29.2 331.5 %all-reduce.2.cloned.1.call-start = ((), (), s32[]{:S(2)}) async-start(), calls=%async_computation.1 | async-start | bytes 524288 | tf_op jit(solution)/shard_map/psum | solution.py:45
  196.9 9.1 %copy-start = (bf16[256,8,16,128]{3,1,2,0:T(8,128)(2,1)S(1)}, bf16[256,8,16,128]{3,1,2,0:T(8,128)(2,1)}, u32[]{:S(2)}) copy-start(bf16[256,8,16,128]{3,1,2,0:T(8,128)(2,1)} %copy.34) | copy-start | bytes 25165828
Sparse Core Ops, SparseCore 0:
  269.4 91.2 all-reduce.1
where the time goes:
time: 370 us; the launch traced here: 369 us
  blocking collectives  158 us (43%)
  waiting for transfers between devices  91.4 us (25%)
  local copies, waits for them, and re-layouts  55.9 us (15%)
  matrix products  42.7 us (12%)
  between operations  13.5 us (4%)
  starting transfers between devices  7.66 us (2%)
    all_gather x1, blocking collectives, on_device(): occ_full = lax.all_gather(g_occ, 'orb', axis=1, tiled=True)  138 us
    psum x1, waiting for transfers between devices, on_device(): whole_sum = lax.psum(partial_value, 'orb')  91.4 us
    reshape x2, local copies, waits for them, and re-layouts, on_device(): product.astype(jnp.bfloat16).reshape(aux_dev, total_rows, tile_width)  24.1 us
    dot_general x2, matrix products, on_device(): jnp.einsum('pmc,qmc->qp', virt_list[moment], occ_prod, preferred_element_...  22.9 us
    all_gather x1, blocking collectives, on_device(): virt_block = lax.all_gather(g_virt, 'aux', axis=2, tiled=True)  20.1 us
    dot_general x2, matrix products, on_device(): jnp.dot(col_dense.reshape(aux_dev * total_rows, tile_width), virt_block[m...  13.6 us
    reshape x1, local copies, waits for them, and re-layouts, on_device(): lax.all_to_all(outgoing, 'orb', split_axis=2, concat_axis=1, tiled=True)  11.8 us
    all_to_all x1, local copies, waits for them, and re-layouts, on_device(): lax.all_to_all(outgoing, 'orb', split_axis=2, concat_axis=1, tiled=True)  9.03 us
  transfers between devices with their start and end apart: 2, of which 1 were waited for; matrix products, arithmetic and copies ran while one was open for 0% of the time, Pallas kernels for 0%

commit v1 on v0

v1 whole, which is shorter than its diff:
```python
import functools
import math

import jax
import jax.numpy as jnp
from jax import lax
from jax.experimental import pallas as pl
from jax.experimental.pallas import tpu as pltpu
from jax.sharding import PartitionSpec as P

MESH = pl.DeviceIdType.MESH
F32 = jnp.float32
BF16 = jnp.bfloat16
CHUNK = 32


def kernel(
    orb,
    aux,
    side,
    scale,
    col_ref,
    live_ref,
    tau_ref,
    occ_ref,
    gv_ref,
    b_ref,
    out_ref,
    stage,
    send,
    recv,
    virt,
    occp,
    kron,
    select,
    occ_mine,
    occ_all,
    gv_mine,
    gv_all,
    gv_both,
    total,
    part,
    shares,
    stage_sem,
    own_sem,
    send_sem,
    recv_sem,
    small_send,
    small_recv,
    share_send,
    share_recv,
):
    me = lax.axis_index("orb")
    my_aux = lax.axis_index("aux")
    chunks = send.shape[0]
    rows = occ_ref.shape[1]
    total_rows = orb * rows
    width = occ_ref.shape[2]
    slots = col_ref.shape[1]
    my_y, my_x = me // side, me % side

    def orb_peer(step):
        step_y, step_x = step // side, step % side
        return lax.rem(my_y + step_y, side) * side + lax.rem(my_x + step_x, side)

    def aux_peer(step):
        return lax.rem(my_aux + step, aux)

    def load(chunk):
        slot = lax.rem(chunk, 2)
        return pltpu.make_async_copy(
            b_ref.at[pl.ds(chunk * CHUNK, CHUNK)], stage.at[slot], stage_sem.at[slot]
        )

    load(0).start()
    load(1).start()
    barrier = pltpu.get_barrier_semaphore()
    for step in range(1, orb):
        pl.semaphore_signal(
            barrier, inc=1, device_id={"orb": orb_peer(step)}, device_id_type=MESH
        )
    for step in range(1, aux):
        pl.semaphore_signal(
            barrier, inc=1, device_id={"aux": aux_peer(step)}, device_id_type=MESH
        )

    lane = lax.broadcasted_iota(jnp.int32, (16 * orb, 128), 1)
    row = lax.broadcasted_iota(jnp.int32, (16 * orb, 128), 0)
    listed = jnp.zeros((16 * orb, 128), jnp.int32)
    for k in range(slots):
        listed = jnp.where(lane % slots == k, col_ref[0, k], listed)
    select[...] = jnp.where(
        (listed == row // 16) & (row % 16 == lane // slots), 1.0, 0.0
    ).astype(BF16)

    lane = lax.broadcasted_iota(jnp.int32, (rows, width), 1)
    for t in range(2):
        live = jnp.zeros((rows, width), jnp.int32)
        for group in range(orb):
            live = jnp.where(lane // rows == group, live_ref[t, me, group], live)
        occ_mine[t] = (occ_ref[t].astype(F32) * live.astype(F32)).astype(BF16)
        gv_mine[t] = gv_ref[t, 0]
    occ_all[me] = occ_mine[...]
    gv_all[my_aux] = gv_mine[...]

    def pack(chunk):
        slot = lax.rem(chunk, 2)
        load(chunk).wait()
        for half in range(CHUNK // 16):
            for pair in range(rows // 2):
                block = [
                    stage[slot, pl.ds(16 * half, 16), 2 * pair + r].reshape(128, width)
                    for r in range(2)
                ]
                picked = jnp.dot(
                    select[...],
                    jnp.concatenate(block, axis=1),
                    preferred_element_type=F32,
                ).reshape(orb, 2, 8, 2 * width)
                picked = jnp.concatenate(
                    [picked[..., :width], picked[..., width:]], axis=2
                )
                send[chunk, :, pl.ds(2 * half, 2), pl.ds(16 * pair, 16), :] = (
                    picked.astype(BF16)
                )

        @pl.when(chunk + 2 < chunks)
        def _():
            load(chunk + 2).start()

    def own(chunk):
        return pltpu.make_async_copy(
            send.at[chunk, me], recv.at[chunk, :, me], own_sem.at[chunk]
        )

    def start(chunk):
        for step in range(1, orb):
            peer = orb_peer(step)
            pltpu.make_async_remote_copy(
                src_ref=send.at[chunk, peer],
                dst_ref=recv.at[chunk, :, me],
                send_sem=send_sem.at[chunk],
                recv_sem=recv_sem.at[chunk],
                device_id={"orb": peer},
                device_id_type=MESH,
            ).start()
        own(chunk).start()

    pack(0)
    pl.semaphore_wait(barrier, orb + aux - 2)
    start(0)
    for step in range(1, orb):
        pltpu.make_async_remote_copy(
            src_ref=occ_mine,
            dst_ref=occ_all.at[me],
            send_sem=small_send.at[0],
            recv_sem=small_recv.at[0],
            device_id={"orb": orb_peer(step)},
            device_id_type=MESH,
        ).start()
    for step in range(1, aux):
        pltpu.make_async_remote_copy(
            src_ref=gv_mine,
            dst_ref=gv_all.at[my_aux],
            send_sem=small_send.at[1],
            recv_sem=small_recv.at[1],
            device_id={"aux": aux_peer(step)},
            device_id_type=MESH,
        ).start()

    def pack_and_start(chunk, carry):
        pack(chunk)
        start(chunk)
        return carry

    lax.fori_loop(1, chunks, pack_and_start, 0)

    def settle(ref, sem):
        pltpu.make_async_copy(ref, ref, sem).wait()

    settle(occ_all.at[pl.ds(0, orb - 1)], small_recv.at[0])
    settle(gv_all.at[pl.ds(0, aux - 1)], small_recv.at[1])

    for t in range(2):
        gv_both[:, pl.ds(t * width, width)] = gv_all[:, t].reshape(width, width)

    deep = 8 * total_rows
    spread = (
        lax.broadcasted_iota(jnp.int32, (total_rows, deep), 1) // 8
        == lax.broadcasted_iota(jnp.int32, (total_rows, deep), 0)
    )
    spread = jnp.where(spread, 1.0, 0.0).astype(BF16)
    same = (
        lax.broadcasted_iota(jnp.int32, (16, 8, deep), 2) % 8
        == lax.broadcasted_iota(jnp.int32, (16, 8, deep), 1)
    )
    for t in range(2):

        def expand(pair, carry, t=t):
            two = occ_all[pl.ds(2 * pair, 2), t].reshape(2 * rows, width)
            wide = jnp.dot(two, spread, preferred_element_type=F32)
            wide = jnp.broadcast_to(wide[:, None, :], (16, 8, deep))
            wide = jnp.where(same, wide, 0.0).astype(BF16).reshape(128, deep)
            kron[pl.ds(pl.multiple_of((t * orb + 2 * pair) * 64, 128), 128), :] = wide
            return carry

        lax.fori_loop(0, orb // 2, expand, 0)

    def consume(chunk, carry):
        own(chunk).wait()
        settle(send.at[chunk, pl.ds(0, orb - 1)], recv_sem.at[chunk])
        for half in range(CHUNK // 16):
            first = chunk * CHUNK + 16 * half
            two = [recv[chunk, 2 * half + i].reshape(deep, width) for i in range(2)]
            place = pl.ds(pl.multiple_of(first, 16), 16)
            product = [
                jnp.dot(rows8, gv_both[...], preferred_element_type=F32).reshape(
                    total_rows, 8, 2 * width
                )
                for rows8 in two
            ]
            product = jnp.concatenate(product, axis=1).astype(BF16)
            virt[0, :, place, :] = product[..., :width]
            virt[1, :, place, :] = product[..., width:]
            both = jnp.concatenate(two, axis=1)
            for t in range(2):
                mixed = jnp.dot(
                    kron[pl.ds(t * deep, deep), :], both, preferred_element_type=F32
                ).reshape(total_rows, 8, 2 * width)
                mixed = jnp.concatenate([mixed[..., :width], mixed[..., width:]], axis=1)
                occp[t, :, place, :] = mixed.astype(BF16)
        return carry

    lax.fori_loop(0, chunks, consume, 0)

    many = 4
    for t in range(2):
        total[...] = jnp.zeros_like(total)

        def contract(block, carry, t=t):
            left = jnp.concatenate([occp[t, many * block + i] for i in range(many)], axis=1)
            right = jnp.concatenate([virt[t, many * block + i] for i in range(many)], axis=1)
            total[...] += lax.dot_general(
                left, right, (((1,), (1,)), ((), ())), preferred_element_type=F32
            )
            return carry

        lax.fori_loop(0, total_rows // many, contract, 0)
        term = (total[...] * tau_ref[t]).reshape(part.shape)
        part[...] = term if t == 0 else (part[...] + term) * scale

    for step in range(1, orb):
        peer = orb_peer(step)
        pltpu.make_async_remote_copy(
            src_ref=part.at[peer],
            dst_ref=shares.at[me],
            send_sem=share_send,
            recv_sem=share_recv,
            device_id={"orb": peer},
            device_id_type=MESH,
        ).start()
    shares[me] = part[me]
    settle(shares.at[pl.ds(0, orb - 1)], share_recv)
    whole = shares[0]
    for group in range(1, orb):
        whole = whole + shares[group]
    out_ref[...] = whole

    settle(shares.at[pl.ds(0, orb - 1)], share_send)
    settle(occ_all.at[pl.ds(0, orb - 1)], small_send.at[0])
    settle(gv_all.at[pl.ds(0, aux - 1)], small_send.at[1])

    def finish(chunk, carry):
        settle(send.at[chunk, pl.ds(0, orb - 1)], send_sem.at[chunk])
        return carry

    lax.fori_loop(0, chunks, finish, 0)


def on_device(b_rows, col_blocks, g_occ, occ_live, g_virt, tau_weight):
    orb, aux = lax.axis_size("orb"), lax.axis_size("aux")
    aux_dev, rows, slots, width = b_rows.shape
    chunks = aux_dev // CHUNK
    total_rows = orb * rows
    deep = 8 * total_rows
    scale = 1.0 / math.sqrt(total_rows * width * orb)
    smem = pl.BlockSpec(memory_space=pltpu.SMEM)
    vmem = pl.BlockSpec(memory_space=pltpu.VMEM)
    share = aux_dev // orb
    dma = pltpu.SemaphoreType.DMA
    return pl.pallas_call(
        functools.partial(kernel, orb, aux, math.isqrt(orb), scale),
        out_shape=jax.ShapeDtypeStruct((share, aux_dev), F32),
        in_specs=[smem, smem, smem, vmem, vmem, pl.BlockSpec(memory_space=pl.ANY)],
        out_specs=vmem,
        scratch_shapes=[
            pltpu.VMEM((2, CHUNK, rows, slots, width), BF16),
            pltpu.VMEM((chunks, orb, CHUNK // 8, 8 * rows, width), BF16),
            pltpu.VMEM((chunks, CHUNK // 8, orb, 8 * rows, width), BF16),
            pltpu.VMEM((2, total_rows, aux_dev, width), BF16),
            pltpu.VMEM((2, total_rows, aux_dev, width), BF16),
            pltpu.VMEM((2 * deep, deep), BF16),
            pltpu.VMEM((16 * orb, 128), BF16),
            pltpu.VMEM((2, rows, width), BF16),
            pltpu.VMEM((orb, 2, rows, width), BF16),
            pltpu.VMEM((2, rows, width), BF16),
            pltpu.VMEM((aux, 2, rows, width), BF16),
            pltpu.VMEM((width, 2 * width), BF16),
            pltpu.VMEM((aux_dev, aux_dev), F32),
            pltpu.VMEM((orb, share, aux_dev), F32),
            pltpu.VMEM((orb, share, aux_dev), F32),
            dma((2,)),
            dma((chunks,)),
            dma((chunks,)),
            dma((chunks,)),
            dma((2,)),
            dma((2,)),
            dma(()),
            dma(()),
        ],
        compiler_params=pltpu.CompilerParams(
            collective_id=0, has_side_effects=True, vmem_limit_bytes=61 * 1024 * 1024
        ),
    )(col_blocks, occ_live, tau_weight, g_occ, g_virt, b_rows)


def solution(mesh):
    in_specs = (
        P("aux", "orb", None, None),
        P("orb", None),
        P(None, "orb", None),
        P(),
        P(None, "orb", "aux", None),
        P(),
    )
    out_specs = P("orb", "aux")
    return jax.shard_map(
        on_device, mesh=mesh, in_specs=in_specs, out_specs=out_specs, check_vma=False
    )
```

time: 370 us -> 137 us (0.37)
  blocking collectives: 158 us -> 0 us
  Pallas kernels: 0 us -> 136 us
  waiting for transfers between devices: 91.4 us -> 0 us
  local copies, waits for them, and re-layouts: 55.9 us -> 1.32 us
  matrix products: 42.7 us -> 0 us
  between operations: 13.5 us -> 0.01 us
  starting transfers between devices: 7.66 us -> 0 us
    all_gather x2 -> x0, blocking collectives: 158 us -> none  [the longest x1 138 us: on_device(): occ_full = lax.all_gather(g_occ, 'orb', axis=1, tiled=True)]
    pallas_call x0 -> x1, Pallas kernels: none -> 136 us  [on_device(): pl.pallas_call(functools.partial(kernel, orb, aux, math.isqrt(orb), scale...]
    psum x1 -> x0, waiting for transfers between devices: 91.4 us -> none  [on_device(): whole_sum = lax.psum(partial_value, 'orb')]
    dot_general x5 -> x0, matrix products: 42.7 us -> none  [the longest x2 22.9 us: on_device(): jnp.einsum('pmc,qmc->qp', virt_list[moment], occ_prod, preferred_element_...]
    reshape x3 -> x0, local copies, waits for them, and re-layouts: 35.9 us -> none  [the longest x2 24.1 us: on_device(): product.astype(jnp.bfloat16).reshape(aux_dev, total_rows, tile_width)]
    all_to_all x1 -> x0, local copies, waits for them, and re-layouts: 9.03 us -> none  [on_device(): lax.all_to_all(outgoing, 'orb', split_axis=2, concat_axis=1, tiled=True)]
    transpose x1 -> x0, local copies, waits for them, and re-layouts: 8.77 us -> none  [on_device(): outgoing = jnp.einsum('prkc,kd->prdc', b_rows, picked)]
    all_to_all x1 -> x0, starting transfers between devices: 7.62 us -> none  [on_device(): lax.all_to_all(outgoing, 'orb', split_axis=2, concat_axis=1, tiled=True)]
  transfers between devices with their start and end apart: 2 -> 0, of which waited for: 1 -> 0; matrix products, arithmetic and copies ran while one was open for 0% -> 0% of each run, Pallas kernels for 0% -> 0%
where the time goes in v1:
time: 137 us
  Pallas kernels  136 us (99%)
    pallas_call x1, Pallas kernels, on_device(): pl.pallas_call(functools.partial(kernel, orb, aux, math.isqrt(orb), scale...  136 us

profile of v1, /device:TPU:2, one launch (start us, length us, event | category | flops | bytes accessed | tf_op | source)
XLA Modules:
  0.0 136.9 jit_solution(1141386062474381798)
XLA Ops:
  0.0 135.5 %shard_map.64 = f32[16,256]{1,0:T(8,128)} custom-call(s32[1,8]{1,0:T(1,128)} %col_ref.1, s32[2,16,16]{2,1,0:T(8,128)} %live_ref.1, f32[2]{0:T(128)} %tau_ref.1, bf16[2,8,128]{2,1,0:T(8,128)(2,1)} %occ_ref.1, bf16[2,1,8,128]{3,2,1,0:T(8,128)(2,1)} %gv_ref.1, bf16[256,8,8,128]{3,2,1,0:T(8,128)(2,1)} %b_ref.1), custom_call_target="tpu_custom_call" | custom-call | tf_op jit(solution)/shard_map/pallas_call | solution.py:291
  135.5 1.3 copy.8

commit v2 on v1

--- a/solution.py
+++ b/solution.py
@@ -11,7 +11,7 @@
 MESH = pl.DeviceIdType.MESH
 F32 = jnp.float32
 BF16 = jnp.bfloat16
-CHUNK = 32
+CHUNK = 16
 
 
 def kernel(
@@ -233,7 +233,7 @@
 
     lax.fori_loop(0, chunks, consume, 0)
 
-    many = 4
+    many = 32
     for t in range(2):
         total[...] = jnp.zeros_like(total)
 

time: 137 us -> 121 us (0.88)
  Pallas kernels: 136 us -> 119 us
    pallas_call x1, Pallas kernels: 136 us -> 119 us  [on_device(): pl.pallas_call(functools.partial(kernel, orb, aux, math.isqrt(orb), scale...]
where the time goes in v2:
time: 121 us; the launch traced here: 120 us
  Pallas kernels  119 us (98%)
  local copies, waits for them, and re-layouts  1.32 us (1%)
    pallas_call x1, Pallas kernels, on_device(): pl.pallas_call(functools.partial(kernel, orb, aux, math.isqrt(orb), scale...  119 us

profile of v2, /device:TPU:2, one launch (start us, length us, event | category | flops | bytes accessed | tf_op | source)
XLA Modules:
  0.0 119.9 jit_solution(16584727082321602628)
XLA Ops:
  0.0 118.6 %shard_map.64 = f32[16,256]{1,0:T(8,128)} custom-call(s32[1,8]{1,0:T(1,128)} %col_ref.1, s32[2,16,16]{2,1,0:T(8,128)} %live_ref.1, f32[2]{0:T(128)} %tau_ref.1, bf16[2,8,128]{2,1,0:T(8,128)(2,1)} %occ_ref.1, bf16[2,1,8,128]{3,2,1,0:T(8,128)(2,1)} %gv_ref.1, bf16[256,8,8,128]{3,2,1,0:T(8,128)(2,1)} %b_ref.1), custom_call_target="tpu_custom_call" | custom-call | tf_op jit(solution)/shard_map/pallas_call | solution.py:291
  118.6 1.3 %copy.8 = f32[16,256]{1,0:T(8,128)} copy(f32[16,256]{1,0:T(8,128)} %shard_map.64) | data formatting | bytes 32768

commit v3 on v2

--- a/solution.py
+++ b/solution.py
@@ -12,6 +12,7 @@
 F32 = jnp.float32
 BF16 = jnp.bfloat16
 CHUNK = 16
+CORES = 2
 
 
 def kernel(
@@ -49,9 +50,14 @@
     small_recv,
     share_send,
     share_recv,
+    pair_sem,
+    down_sem,
+    up_sem,
 ):
     me = lax.axis_index("orb")
     my_aux = lax.axis_index("aux")
+    planes = aux // CORES
+    my_z, my_core = my_aux // CORES, my_aux % CORES
     chunks = send.shape[0]
     rows = occ_ref.shape[1]
     total_rows = orb * rows
@@ -63,8 +69,8 @@
         step_y, step_x = step // side, step % side
         return lax.rem(my_y + step_y, side) * side + lax.rem(my_x + step_x, side)
 
-    def aux_peer(step):
-        return lax.rem(my_aux + step, aux)
+    def at(z, core):
+        return {"aux": z * CORES + core}
 
     def load(chunk):
         slot = lax.rem(chunk, 2)
@@ -79,10 +85,11 @@
         pl.semaphore_signal(
             barrier, inc=1, device_id={"orb": orb_peer(step)}, device_id_type=MESH
         )
-    for step in range(1, aux):
-        pl.semaphore_signal(
-            barrier, inc=1, device_id={"aux": aux_peer(step)}, device_id_type=MESH
-        )
+    for ahead, target in ((my_z < planes - 1, at(my_z + 1, my_core)), (my_core == 0, at(my_z, 1))):
+
+        @pl.when(ahead)
+        def _(target=target):
+            pl.semaphore_signal(barrier, inc=1, device_id=target, device_id_type=MESH)
 
     lane = lax.broadcasted_iota(jnp.int32, (16 * orb, 128), 1)
     row = lax.broadcasted_iota(jnp.int32, (16 * orb, 128), 0)
@@ -101,7 +108,7 @@
         occ_mine[t] = (occ_ref[t].astype(F32) * live.astype(F32)).astype(BF16)
         gv_mine[t] = gv_ref[t, 0]
     occ_all[me] = occ_mine[...]
-    gv_all[my_aux] = gv_mine[...]
+    gv_all[my_core, my_z] = gv_mine[...]
 
     def pack(chunk):
         slot = lax.rem(chunk, 2)
@@ -147,7 +154,7 @@
         own(chunk).start()
 
     pack(0)
-    pl.semaphore_wait(barrier, orb + aux - 2)
+    pl.semaphore_wait(barrier, orb - 1 + jnp.minimum(my_z, 1) + my_core)
     start(0)
     for step in range(1, orb):
         pltpu.make_async_remote_copy(
@@ -158,16 +165,6 @@
             device_id={"orb": orb_peer(step)},
             device_id_type=MESH,
         ).start()
-    for step in range(1, aux):
-        pltpu.make_async_remote_copy(
-            src_ref=gv_mine,
-            dst_ref=gv_all.at[my_aux],
-            send_sem=small_send.at[1],
-            recv_sem=small_recv.at[1],
-            device_id={"aux": aux_peer(step)},
-            device_id_type=MESH,
-        ).start()
-
     def pack_and_start(chunk, carry):
         pack(chunk)
         start(chunk)
@@ -179,10 +176,53 @@
         pltpu.make_async_copy(ref, ref, sem).wait()
 
     settle(occ_all.at[pl.ds(0, orb - 1)], small_recv.at[0])
-    settle(gv_all.at[pl.ds(0, aux - 1)], small_recv.at[1])
-
+
+    @pl.when(my_core == 1)
+    def _():
+        pl.semaphore_signal(pair_sem, inc=1, device_id=at(my_z, 0), device_id_type=MESH)
+
+    @pl.when(my_core == 0)
+    def _():
+        pl.semaphore_wait(pair_sem, 1)
+
+    for sem, waits, sends, target in (
+        (down_sem, my_z < planes - 1, my_z > 0, at(my_z - 1, my_core)),
+        (up_sem, my_z > 0, my_z < planes - 1, at(my_z + 1, my_core)),
+    ):
+
+        @pl.when(waits)
+        def _(sem=sem):
+            pl.semaphore_wait(sem, 1)
+
+        @pl.when(sends)
+        def _(sem=sem, target=target):
+            pl.semaphore_signal(sem, inc=1, device_id=target, device_id_type=MESH)
+
+    for step in range(1, planes):
+        pltpu.make_async_remote_copy(
+            src_ref=gv_mine,
+            dst_ref=gv_all.at[my_core, my_z],
+            send_sem=small_send.at[1],
+            recv_sem=small_recv.at[1],
+            device_id=at(lax.rem(my_z + step, planes), my_core),
+            device_id_type=MESH,
+        ).start()
+    settle(gv_all.at[0, pl.ds(0, planes - 1)], small_recv.at[1])
+    swap = pltpu.make_async_remote_copy(
+        src_ref=gv_all.at[my_core],
+        dst_ref=gv_all.at[my_core],
+        send_sem=small_send.at[2],
+        recv_sem=small_recv.at[2],
+        device_id=at(my_z, 1 - my_core),
+        device_id_type=MESH,
+    )
+    swap.start()
+    swap.wait()
     for t in range(2):
-        gv_both[:, pl.ds(t * width, width)] = gv_all[:, t].reshape(width, width)
+        for z in range(planes):
+            for core in range(CORES):
+                place = pl.ds((z * CORES + core) * rows, rows)
+                gv_both[place, pl.ds(t * width, width)] = gv_all[core, z, t]
 
     deep = 8 * total_rows
     spread = (
@@ -233,7 +273,7 @@
 
     lax.fori_loop(0, chunks, consume, 0)
 
-    many = 32
+    many = 64
     for t in range(2):
         total[...] = jnp.zeros_like(total)
 
@@ -268,7 +308,7 @@
 
     settle(shares.at[pl.ds(0, orb - 1)], share_send)
     settle(occ_all.at[pl.ds(0, orb - 1)], small_send.at[0])
-    settle(gv_all.at[pl.ds(0, aux - 1)], small_send.at[1])
+    settle(gv_all.at[0, pl.ds(0, planes - 1)], small_send.at[1])
 
     def finish(chunk, carry):
         settle(send.at[chunk, pl.ds(0, orb - 1)], send_sem.at[chunk])
@@ -304,7 +344,7 @@
             pltpu.VMEM((2, rows, width), BF16),
             pltpu.VMEM((orb, 2, rows, width), BF16),
             pltpu.VMEM((2, rows, width), BF16),
-            pltpu.VMEM((aux, 2, rows, width), BF16),
+            pltpu.VMEM((CORES, aux // CORES, 2, rows, width), BF16),
             pltpu.VMEM((width, 2 * width), BF16),
             pltpu.VMEM((aux_dev, aux_dev), F32),
             pltpu.VMEM((orb, share, aux_dev), F32),
@@ -313,10 +353,13 @@
             dma((chunks,)),
             dma((chunks,)),
             dma((chunks,)),
-            dma((2,)),
-            dma((2,)),
+            dma((3,)),
+            dma((3,)),
             dma(()),
             dma(()),
+            pltpu.SemaphoreType.REGULAR,
+            pltpu.SemaphoreType.REGULAR,
+            pltpu.SemaphoreType.REGULAR,
         ],
         compiler_params=pltpu.CompilerParams(
             collective_id=0, has_side_effects=True, vmem_limit_bytes=61 * 1024 * 1024

time: 121 us -> 115 us (0.950)
  Pallas kernels: 119 us -> 113 us
    pallas_call x1, Pallas kernels: 119 us -> 113 us  [on_device(): pl.pallas_call(functools.partial(kernel, orb, aux, math.isqrt(orb), scale...]
where the time goes in v3:
time: 115 us; the launch traced here: 114 us
  Pallas kernels  113 us (98%)
  local copies, waits for them, and re-layouts  1.32 us (1%)
    pallas_call x1, Pallas kernels, on_device(): pl.pallas_call(functools.partial(kernel, orb, aux, math.isqrt(orb), scale...  113 us

profile of v3, /device:TPU:2, one launch (start us, length us, event | category | flops | bytes accessed | tf_op | source)
XLA Modules:
  0.0 114.0 jit_solution(8047644887795503685)
XLA Ops:
  0.0 112.7 %shard_map.64 = f32[16,256]{1,0:T(8,128)} custom-call(s32[1,8]{1,0:T(1,128)} %col_ref.1, s32[2,16,16]{2,1,0:T(8,128)} %live_ref.1, f32[2]{0:T(128)} %tau_ref.1, bf16[2,8,128]{2,1,0:T(8,128)(2,1)} %occ_ref.1, bf16[2,1,8,128]{3,2,1,0:T(8,128)(2,1)} %gv_ref.1, bf16[256,8,8,128]{3,2,1,0:T(8,128)(2,1)} %b_ref.1), custom_call_target="tpu_custom_call" | custom-call | tf_op jit(solution)/shard_map/pallas_call | solution.py:331
  112.7 1.3 %copy.8 = f32[16,256]{1,0:T(8,128)} copy(f32[16,256]{1,0:T(8,128)} %shard_map.64) | data formatting | bytes 32768

commit v4 on v3

--- a/solution.py
+++ b/solution.py
@@ -20,13 +20,17 @@
     aux,
     side,
     scale,
+    col_hbm,
+    live_hbm,
+    tau_hbm,
+    occ_hbm,
+    gv_hbm,
+    b_ref,
+    out_ref,
     col_ref,
     live_ref,
     tau_ref,
     occ_ref,
-    gv_ref,
-    b_ref,
-    out_ref,
     stage,
     send,
     recv,
@@ -42,6 +46,7 @@
     total,
     part,
     shares,
+    small_sem,
     stage_sem,
     own_sem,
     send_sem,
@@ -78,8 +83,12 @@
             b_ref.at[pl.ds(chunk * CHUNK, CHUNK)], stage.at[slot], stage_sem.at[slot]
         )
 
+    def small(i):
+        pairs = ((col_hbm, col_ref), (live_hbm, live_ref), (tau_hbm, tau_ref), (occ_hbm, occ_ref), (gv_hbm, gv_mine))
+        return pltpu.make_async_copy(*pairs[i], small_sem.at[i])
+
+    small(0).start()
     load(0).start()
-    load(1).start()
     barrier = pltpu.get_barrier_semaphore()
     for step in range(1, orb):
         pl.semaphore_signal(
@@ -90,6 +99,11 @@
         @pl.when(ahead)
         def _(target=target):
             pl.semaphore_signal(barrier, inc=1, device_id=target, device_id_type=MESH)
+
+    load(1).start()
+    for i in range(1, 5):
+        small(i).start()
+    small(0).wait()
 
     lane = lax.broadcasted_iota(jnp.int32, (16 * orb, 128), 1)
     row = lax.broadcasted_iota(jnp.int32, (16 * orb, 128), 0)
@@ -99,16 +113,6 @@
     select[...] = jnp.where(
         (listed == row // 16) & (row % 16 == lane // slots), 1.0, 0.0
     ).astype(BF16)
-
-    lane = lax.broadcasted_iota(jnp.int32, (rows, width), 1)
-    for t in range(2):
-        live = jnp.zeros((rows, width), jnp.int32)
-        for group in range(orb):
-            live = jnp.where(lane // rows == group, live_ref[t, me, group], live)
-        occ_mine[t] = (occ_ref[t].astype(F32) * live.astype(F32)).astype(BF16)
-        gv_mine[t] = gv_ref[t, 0]
-    occ_all[me] = occ_mine[...]
-    gv_all[my_core, my_z] = gv_mine[...]
 
     def pack(chunk):
         slot = lax.rem(chunk, 2)
@@ -156,6 +160,17 @@
     pack(0)
     pl.semaphore_wait(barrier, orb - 1 + jnp.minimum(my_z, 1) + my_core)
     start(0)
+    for i in range(1, 5):
+        small(i).wait()
+    lane = lax.broadcasted_iota(jnp.int32, (rows, width), 1)
+    for t in range(2):
+        live = jnp.zeros((rows, width), jnp.int32)
+        for group in range(orb):
+            live = jnp.where(lane // rows == group, live_ref[t, me, group], live)
+        occ_mine[t] = (occ_ref[t].astype(F32) * live.astype(F32)).astype(BF16)
+    occ_all[me] = occ_mine[...]
+    gv_all[my_core, my_z] = gv_mine[...]
+
     for step in range(1, orb):
         pltpu.make_async_remote_copy(
             src_ref=occ_mine,
@@ -222,7 +237,7 @@
         for z in range(planes):
             for core in range(CORES):
                 place = pl.ds((z * CORES + core) * rows, rows)
-                gv_both[place, pl.ds(t * width, width)] = gv_all[core, z, t]
+                gv_both[place, pl.ds(t * width, width)] = gv_all[core, z, t, 0]
 
     deep = 8 * total_rows
     spread = (
@@ -273,24 +288,22 @@
 
     lax.fori_loop(0, chunks, consume, 0)
 
-    many = 64
     for t in range(2):
-        total[...] = jnp.zeros_like(total)
-
-        def contract(block, carry, t=t):
-            left = jnp.concatenate([occp[t, many * block + i] for i in range(many)], axis=1)
-            right = jnp.concatenate([virt[t, many * block + i] for i in range(many)], axis=1)
-            total[...] += lax.dot_general(
-                left, right, (((1,), (1,)), ((), ())), preferred_element_type=F32
-            )
-            return carry
-
-        lax.fori_loop(0, total_rows // many, contract, 0)
-        term = (total[...] * tau_ref[t]).reshape(part.shape)
-        part[...] = term if t == 0 else (part[...] + term) * scale
-
-    for step in range(1, orb):
+        left = jnp.concatenate([occp[t, m] for m in range(total_rows)], axis=1)
+        right = jnp.concatenate([virt[t, m] for m in range(total_rows)], axis=1)
+        total[t] = lax.dot_general(
+            left, right, (((1,), (1,)), ((), ())), preferred_element_type=F32
+        ).reshape(part.shape)
+
+    def weigh(peer):
+        part[peer] = (total[0, peer] * tau_ref[0] + total[1, peer] * tau_ref[1]) * scale
+
+    def hops(step):
+        return sum(min(n, side - n) for n in (step // side, step % side))
+
+    for step in sorted(range(1, orb), key=hops, reverse=True):
         peer = orb_peer(step)
+        weigh(peer)
         pltpu.make_async_remote_copy(
             src_ref=part.at[peer],
             dst_ref=shares.at[me],
@@ -299,6 +312,7 @@
             device_id={"orb": peer},
             device_id_type=MESH,
         ).start()
+    weigh(me)
     shares[me] = part[me]
     settle(shares.at[pl.ds(0, orb - 1)], share_recv)
     whole = shares[0]
@@ -324,16 +338,19 @@
     total_rows = orb * rows
     deep = 8 * total_rows
     scale = 1.0 / math.sqrt(total_rows * width * orb)
-    smem = pl.BlockSpec(memory_space=pltpu.SMEM)
     vmem = pl.BlockSpec(memory_space=pltpu.VMEM)
     share = aux_dev // orb
     dma = pltpu.SemaphoreType.DMA
     return pl.pallas_call(
         functools.partial(kernel, orb, aux, math.isqrt(orb), scale),
         out_shape=jax.ShapeDtypeStruct((share, aux_dev), F32),
-        in_specs=[smem, smem, smem, vmem, vmem, pl.BlockSpec(memory_space=pl.ANY)],
+        in_specs=[pl.BlockSpec(memory_space=pltpu.HBM)] * 6,
         out_specs=vmem,
         scratch_shapes=[
+            pltpu.SMEM(col_blocks.shape, jnp.int32),
+            pltpu.SMEM(occ_live.shape, jnp.int32),
+            pltpu.SMEM(tau_weight.shape, F32),
+            pltpu.VMEM(g_occ.shape, BF16),
             pltpu.VMEM((2, CHUNK, rows, slots, width), BF16),
             pltpu.VMEM((chunks, orb, CHUNK // 8, 8 * rows, width), BF16),
             pltpu.VMEM((chunks, CHUNK // 8, orb, 8 * rows, width), BF16),
@@ -343,12 +360,13 @@
             pltpu.VMEM((16 * orb, 128), BF16),
             pltpu.VMEM((2, rows, width), BF16),
             pltpu.VMEM((orb, 2, rows, width), BF16),
-            pltpu.VMEM((2, rows, width), BF16),
-            pltpu.VMEM((CORES, aux // CORES, 2, rows, width), BF16),
+            pltpu.VMEM(g_virt.shape, BF16),
+            pltpu.VMEM((CORES, aux // CORES, *g_virt.shape), BF16),
             pltpu.VMEM((width, 2 * width), BF16),
-            pltpu.VMEM((aux_dev, aux_dev), F32),
+            pltpu.VMEM((2, orb, share, aux_dev), F32),
             pltpu.VMEM((orb, share, aux_dev), F32),
             pltpu.VMEM((orb, share, aux_dev), F32),
+            dma((5,)),
             dma((2,)),
             dma((chunks,)),
             dma((chunks,)),

time: 115 us -> 114 us (level)
  Pallas kernels: 113 us -> 111 us
    pallas_call x1, Pallas kernels: 113 us -> 111 us  [on_device(): pl.pallas_call(functools.partial(kernel, orb, aux, math.isqrt(orb), scale...]
where the time goes in v4:
time: 114 us; the launch traced here: 112 us
  Pallas kernels  111 us (97%)
  local copies, waits for them, and re-layouts  1.32 us (1%)
    pallas_call x1, Pallas kernels, on_device(): pl.pallas_call(functools.partial(kernel, orb, aux, math.isqrt(orb), scale...  111 us

profile of v4, /device:TPU:2, one launch (start us, length us, event | category | flops | bytes accessed | tf_op | source)
XLA Modules:
  0.0 112.4 jit_solution(6047509153073129211)
XLA Ops:
  0.0 111.1 %shard_map.64 = f32[16,256]{1,0:T(8,128)} custom-call(s32[1,8]{1,0:T(1,128)} %col_hbm.1, s32[2,16,16]{2,1,0:T(8,128)} %live_hbm.1, f32[2]{0:T(128)} %tau_hbm.1, bf16[2,8,128]{2,1,0:T(8,128)(2,1)} %occ_hbm.1, bf16[2,1,8,128]{3,2,1,0:T(8,128)(2,1)} %gv_hbm.1, bf16[256,8,8,128]{3,2,1,0:T(8,128)(2,1)} %b_ref.1), custom_call_target="tpu_custom_call" | custom-call | tf_op jit(solution)/shard_map/pallas_call | solution.py:344
  111.1 1.3 %copy.8 = f32[16,256]{1,0:T(8,128)} copy(f32[16,256]{1,0:T(8,128)} %shard_map.64) | data formatting | bytes 32768

commit v5 on v4

--- a/solution.py
+++ b/solution.py
@@ -12,6 +12,7 @@
 F32 = jnp.float32
 BF16 = jnp.bfloat16
 CHUNK = 16
+ORDER = [10, 1, 15, 4, 9, 3, 6, 12, 5, 11, 2, 14, 8, 7, 13]
 CORES = 2
 
 
@@ -145,7 +146,7 @@
         )
 
     def start(chunk):
-        for step in range(1, orb):
+        for step in ORDER:
             peer = orb_peer(step)
             pltpu.make_async_remote_copy(
                 src_ref=send.at[chunk, peer],

time: 114 us -> 113 us (level)
  no operation moved by 1% of the time
where the time goes in v5:
time: 113 us; the launch traced here: 112 us
  Pallas kernels  111 us (98%)
  local copies, waits for them, and re-layouts  1.32 us (1%)
    pallas_call x1, Pallas kernels, on_device(): pl.pallas_call(functools.partial(kernel, orb, aux, math.isqrt(orb), scale...  111 us

profile of v5, /device:TPU:2, one launch (start us, length us, event | category | flops | bytes accessed | tf_op | source)
XLA Modules:
  0.0 111.9 jit_solution(12601126826350253656)
XLA Ops:
  0.0 110.5 %shard_map.64 = f32[16,256]{1,0:T(8,128)} custom-call(s32[1,8]{1,0:T(1,128)} %col_hbm.1, s32[2,16,16]{2,1,0:T(8,128)} %live_hbm.1, f32[2]{0:T(128)} %tau_hbm.1, bf16[2,8,128]{2,1,0:T(8,128)(2,1)} %occ_hbm.1, bf16[2,1,8,128]{3,2,1,0:T(8,128)(2,1)} %gv_hbm.1, bf16[256,8,8,128]{3,2,1,0:T(8,128)(2,1)} %b_ref.1), custom_call_target="tpu_custom_call" | custom-call | tf_op jit(solution)/shard_map/pallas_call | solution.py:345
  110.5 1.3 %copy.8 = f32[16,256]{1,0:T(8,128)} copy(f32[16,256]{1,0:T(8,128)} %shard_map.64) | data formatting | bytes 32768

commit v6 on v5

--- a/solution.py
+++ b/solution.py
@@ -279,12 +279,11 @@
             virt[0, :, place, :] = product[..., :width]
             virt[1, :, place, :] = product[..., width:]
             both = jnp.concatenate(two, axis=1)
-            for t in range(2):
-                mixed = jnp.dot(
-                    kron[pl.ds(t * deep, deep), :], both, preferred_element_type=F32
-                ).reshape(total_rows, 8, 2 * width)
-                mixed = jnp.concatenate([mixed[..., :width], mixed[..., width:]], axis=1)
-                occp[t, :, place, :] = mixed.astype(BF16)
+            mixed = jnp.dot(kron[...], both, preferred_element_type=F32).reshape(
+                2, total_rows, 8, 2 * width
+            )
+            mixed = jnp.concatenate([mixed[..., :width], mixed[..., width:]], axis=2)
+            occp[:, :, place, :] = mixed.astype(BF16)
         return carry
 
     lax.fori_loop(0, chunks, consume, 0)

time: 113 us -> 113 us (level)
  no operation moved by 1% of the time
where the time goes in v6:
time: 113 us; the launch traced here: 112 us
  Pallas kernels  111 us (98%)
  local copies, waits for them, and re-layouts  1.32 us (1%)
    pallas_call x1, Pallas kernels, on_device(): pl.pallas_call(functools.partial(kernel, orb, aux, math.isqrt(orb), scale...  111 us

profile of v6, /device:TPU:2, one launch (start us, length us, event | category | flops | bytes accessed | tf_op | source)
XLA Modules:
  0.0 111.9 jit_solution(15785510679030701792)
XLA Ops:
  0.0 110.5 %shard_map.64 = f32[16,256]{1,0:T(8,128)} custom-call(s32[1,8]{1,0:T(1,128)} %col_hbm.1, s32[2,16,16]{2,1,0:T(8,128)} %live_hbm.1, f32[2]{0:T(128)} %tau_hbm.1, bf16[2,8,128]{2,1,0:T(8,128)(2,1)} %occ_hbm.1, bf16[2,1,8,128]{3,2,1,0:T(8,128)(2,1)} %gv_hbm.1, bf16[256,8,8,128]{3,2,1,0:T(8,128)(2,1)} %b_ref.1), custom_call_target="tpu_custom_call" | custom-call | tf_op jit(solution)/shard_map/pallas_call | solution.py:344
  110.5 1.3 %copy.8 = f32[16,256]{1,0:T(8,128)} copy(f32[16,256]{1,0:T(8,128)} %shard_map.64) | data formatting | bytes 32768
